TPU v7x, 32 devices: a whole 2x2x4 slice. The times are simulated.
32 devices in a mesh: row: 4 (over y, x), col: 8 (over z, core).
Axes of the slice: x: 2, y: 2, z: 4, core: 2. Of those that a mesh axis runs over, the one named last changes fastest.
Arguments:
- panel_right: bfloat16 [32, 1536, 128], P('row', 'col'), may hold values from -1 to 1
- factor_inverse: bfloat16 [1536, 1536], replicated, as said below
- ranks: int32 [32], P(('row', 'col')), may hold values from 32 to 128
- owner_map: int32 [32], replicated, may hold values from 0 to 31, each once
- cores: float32 [4, 8, 8, 4, 128, 128], P('row', 'col'), may hold values from -6 to 6
Outputs:
- new_cores: float32 [4, 8, 8, 4, 128, 128], P('row', 'col')
Inputs may be any that keep to these rules, and one draw needn't show every extreme that they name: `factor_inverse`: lower triangular, the inverse of a Cholesky factor.
All inputs are finite; a program needn't handle non-finite values.
Results may differ from a plain program's by a relative error of at most 0.0033.
Values may be sent and summed in bfloat16 or wider, within the bound.
No kernel may reach another device: no remote copies, remote signals or barrier semaphores. Data moves between devices by JAX's collectives and lax.ppermute only.
A program may use at most 128 MiB of HBM per device.

v0:
```python
import jax
import jax.numpy as jnp
from jax import lax
from jax.sharding import PartitionSpec as P


def body(panel_right, factor_inverse, ranks, owner_map, cores):
    n_row = lax.axis_size("row")
    n_col = lax.axis_size("col")
    devices = n_row * n_col
    order = factor_inverse.shape[0]
    width = panel_right.shape[2]
    whole = lax.all_to_all(panel_right, "col", split_axis=0, concat_axis=1, tiled=True)
    solved = jnp.einsum("ij,bjk->bik", factor_inverse, whole, preferred_element_type=jnp.float32)
    column = lax.broadcasted_iota(jnp.int32, (1, 1, width), 2)
    keep = column < ranks.reshape(1, 1, 1)
    panel_left = jnp.where(keep, solved, 0.0).astype(jnp.bfloat16)
    pieces = panel_left.reshape(devices, order // devices, width)
    spread = lax.all_to_all(pieces, ("row", "col"), split_axis=0, concat_axis=0, tiled=True)
    moved = jnp.take(spread, owner_map, axis=0)
    back = lax.all_to_all(moved, ("row", "col"), split_axis=0, concat_axis=0, tiled=True)
    held = back.reshape(1, order, width)
    column_set = lax.all_gather(held, "row", axis=0, tiled=True)
    gram = jnp.einsum(
        "aik,bil->abkl",
        lax.all_gather(held, "col", axis=0, tiled=True),
        column_set,
        preferred_element_type=jnp.float32,
    )
    return cores - gram[None, None]


def solution(mesh):
    return jax.shard_map(
        body,
        mesh=mesh,
        in_specs=(
            P("row", "col", None),
            P(),
            P(("row", "col")),
            P(),
            P("row", "col", None, None, None, None),
        ),
        out_specs=P("row", "col", None, None, None, None),
        check_vma=False,
    )
```

profile of v0, /device:TPU:0, one launch (start us, length us, event | category | flops | bytes accessed | tf_op | source)
XLA Modules:
  0.0 147.6 jit_solution(1991811806430617758)
XLA Ops:
  6.5 6.4 %all-to-all-start = ((bf16[8,192,128]{2,1,0:T(8,128)(2,1)}), bf16[8,192,128]{2,1,0:T(8,128)(2,1)S(1)}, u32[]{:S(2)}, u32[]{:S(2)}) async-start(bf16[8,192,128]{2,1,0:T(8,128)(2,1)} %param.5), calls=%async_computation | async-start | bytes 786432 | tf_op jit(solution)/shard_map/all_to_all | solution.py:13
  13.6 11.9 %all-to-all-done = bf16[8,192,128]{2,1,0:T(8,128)(2,1)S(1)} async-done(((bf16[8,192,128]{2,1,0:T(8,128)(2,1)}), bf16[8,192,128]{2,1,0:T(8,128)(2,1)S(1)}, u32[]{:S(2)}, u32[]{:S(2)}) %all-to-all-start) | async-done | bytes 393248 | tf_op jit(solution)/shard_map/all_to_all | solution.py:13
  25.4 0.0 copy-start
  25.4 4.0 %fusion.4 = bf16[1,1536,128]{1,2,0:T(8,128)(2,1)S(1)} fusion(bf16[1536,128]{1,0:T(8,128)(2,1)S(1)} %bitcast.33, bf16[1536,1536]{1,0:T(8,128)(2,1)} %param.6, pred[128]{0:T(512)(128)(4,1)S(1)} %iota_compare_fusion), kind=kOutput, calls=%fused_computation.6 | convolution fusion | flops 604372992 | bytes 5505152 | tf_op jit(solution)/shard_map/ij,bjk->bik/dot_general | solution.py:14
  29.4 0.9 copy.14
  30.4 3.5 %all-to-all-start.1 = ((bf16[32,48,128]{2,1,0:T(8,128)(2,1)}), bf16[32,48,128]{2,1,0:T(8,128)(2,1)S(1)}, u32[]{:S(2)}, u32[]{:S(2)}) async-start(bf16[32,48,128]{2,1,0:T(8,128)(2,1)} %bitcast.4), calls=%async_computation.1 | async-start | bytes 786432 | tf_op jit(solution)/shard_map/all_to_all | solution.py:19
  33.9 0.0 all-gather.3.cloned.1.call-start
  34.0 0.0 copy-done
  34.0 13.3 %all-to-all-done.1 = bf16[32,48,128]{2,1,0:T(8,128)(2,1)S(1)} async-done(((bf16[32,48,128]{2,1,0:T(8,128)(2,1)}), bf16[32,48,128]{2,1,0:T(8,128)(2,1)S(1)}, u32[]{:S(2)}, u32[]{:S(2)}) %all-to-all-start.1) | async-done | bytes 393248 | tf_op jit(solution)/shard_map/all_to_all | solution.py:19
  47.3 0.6 gather_fusion
  48.0 0.1 broadcast_select_fusion
  48.1 15.8 %all_to_all.19 = bf16[32,48,128]{2,1,0:T(8,128)(2,1)} all-to-all(bf16[32,48,128]{2,1,0:T(8,128)(2,1)S(1)} %broadcast_select_fusion), channel_id=1, replica_groups=mesh['row'=4,'col'=8] {'row','col'}, dimensions={0} | all-to-all | bytes 786432 | tf_op jit(solution)/shard_map/all_to_all | solution.py:21
  63.9 0.0 all-gather.3.cloned.1.call-update
  63.9 0.0 all-gather.5.cloned.1.call-start
  64.0 0.7 all-gather.5.cloned.1.call-update
  64.7 1.9 %copy.16 = f32[1,1,8,4,128,128]{4,5,2,3,1,0:T(8,128)S(1)} copy(f32[1,1,8,4,128,128]{5,4,3,2,1,0:T(8,128)} %param.9) | data formatting | bytes 4194304 | tf_op args[4]
  66.6 25.9 %all-gather.3.cloned.1.call-done = bf16[4,1536,128]{2,1,0:T(8,128)(2,1)} async-done(((bf16[1,1536,128]{2,1,0:T(8,128)(2,1)}), bf16[4,1536,128]{2,1,0:T(8,128)(2,1)}) %all-gather.3.cloned.1.call-update) | async-done | bytes 1572880 | tf_op jit(solution)/shard_map/all_gather | solution.py:23
  92.5 39.9 %all-gather.5.cloned.1.call-done = bf16[8,1536,128]{2,1,0:T(8,128)(2,1)} async-done(((bf16[1,1536,128]{2,1,0:T(8,128)(2,1)}), bf16[8,1536,128]{2,1,0:T(8,128)(2,1)}) %all-gather.5.cloned.1.call-update) | async-done | bytes 3145744 | tf_op jit(solution)/shard_map/all_gather | solution.py:26
  132.4 5.5 %bitcast_subtract_fusion = f32[1,1,8,4,128,128]{4,5,2,3,1,0:T(8,128)} fusion(f32[1,1,8,4,128,128]{4,5,2,3,1,0:T(8,128)S(1)} %copy.16, bf16[8,1536,128]{2,1,0:T(8,128)(2,1)} %all-gather.5.cloned.1.call-done, bf16[4,1536,128]{2,1,0:T(8,128)(2,1)} %all-gather.3.cloned.1.call-done), kind=kOutput, calls=%fused_computation.7 | convolution fusion | flops 1611137024 | bytes 8912896 | tf_op jit(solution)/shard_map/aik,bil->abkl/dot_general | solution.py:24
  137.9 2.9 %copy.17 = f32[1,1,8,4,128,128]{5,4,3,2,1,0:T(8,128)} copy(f32[1,1,8,4,128,128]{4,5,2,3,1,0:T(8,128)} %bitcast_subtract_fusion) | data formatting | bytes 4194304 | tf_op jit(solution)/shard_map/sub | solution.py:30
  (4 shorter events, 0.0 us)
Async XLA Ops:
  6.5 18.9 %all-to-all-start = ((bf16[8,192,128]{2,1,0:T(8,128)(2,1)}), bf16[8,192,128]{2,1,0:T(8,128)(2,1)S(1)}, u32[]{:S(2)}, u32[]{:S(2)}) async-start(bf16[8,192,128]{2,1,0:T(8,128)(2,1)} %param.5), calls=%async_computation | async-start | bytes 786432 | tf_op jit(solution)/shard_map/all_to_all | solution.py:13
  25.4 8.6 %copy-start = (s32[32]{0:T(128)S(1)}, s32[32]{0:T(128)}, u32[]{:S(2)}) copy-start(s32[32]{0:T(128)} %param.8) | copy-start | bytes 388
  30.4 17.0 %all-to-all-start.1 = ((bf16[32,48,128]{2,1,0:T(8,128)(2,1)}), bf16[32,48,128]{2,1,0:T(8,128)(2,1)S(1)}, u32[]{:S(2)}, u32[]{:S(2)}) async-start(bf16[32,48,128]{2,1,0:T(8,128)(2,1)} %bitcast.4), calls=%async_computation.1 | async-start | bytes 786432 | tf_op jit(solution)/shard_map/all_to_all | solution.py:19
  33.9 58.6 %all-gather.3.cloned.1.call-start = ((), (), s32[]{:S(2)}) async-start(), calls=%async_computation.3 | async-start | bytes 1966080 | tf_op jit(solution)/shard_map/all_gather | solution.py:23
  63.9 68.5 %all-gather.5.cloned.1.call-start = ((), (), s32[]{:S(2)}) async-start(), calls=%async_computation.4 | async-start | bytes 3538944 | tf_op jit(solution)/shard_map/all_gather | solution.py:26
Sparse Core Ops, SparseCore 0:
  64.0 28.4 all-gather.2
  94.1 38.2 all-gather.4
where the time goes:
time: 148 us
  waiting for transfers between devices  91.7 us (62%)
  blocking collectives  15.8 us (11%)
  between operations  14.1 us (10%)
  starting transfers between devices  9.97 us (7%)
  matrix products  9.54 us (6%)
  local copies, waits for them, and re-layouts  6.37 us (4%)
    all_gather x1, waiting for transfers between devices, body(): lax.all_gather(held, 'col', axis=0, tiled=True)  39.9 us
    all_gather x1, waiting for transfers between devices, body(): column_set = lax.all_gather(held, 'row', axis=0, tiled=True)  25.9 us
    all_to_all x1, blocking collectives, body(): lax.all_to_all(moved, ('row', 'col'), split_axis=0, concat_axis=0, tiled=...  15.8 us
    all_to_all x1, waiting for transfers between devices, body(): lax.all_to_all(pieces, ('row', 'col'), split_axis=0, concat_axis=0, tiled...  13.3 us
    all_to_all x1, waiting for transfers between devices, body(): lax.all_to_all(panel_right, 'col', split_axis=0, concat_axis=1, tiled=True)  11.9 us
    all_to_all x1, starting transfers between devices, body(): lax.all_to_all(panel_right, 'col', split_axis=0, concat_axis=1, tiled=True)  6.35 us
    dot_general x1, matrix products, body(): jnp.einsum('aik,bil->abkl', lax.all_gather(held, 'col', axis=0, tiled=Tru...  5.51 us
    dot_general x1, matrix products, body(): jnp.einsum('ij,bjk->bik', factor_inverse, whole, preferred_element_type=j...  4.03 us
  transfers between devices with their start and end apart: 4, of which 4 were waited for; matrix products, arithmetic and copies ran while one was open for 1% of the time, Pallas kernels for 0%

commit v1 on v0

--- a/solution.py
+++ b/solution.py
@@ -2,6 +2,12 @@
 import jax.numpy as jnp
 from jax import lax
 from jax.sharding import PartitionSpec as P
+
+
+def swap_blocks(x, axis, split, join):
+    shards = jnp.split(x, lax.axis_size(axis), axis=split)
+    received = lax.all_to_all(jnp.stack(shards), axis, 0, 0)
+    return jnp.concatenate(received, axis=join)
 
 
 def body(panel_right, factor_inverse, ranks, owner_map, cores):
@@ -10,7 +16,7 @@
     devices = n_row * n_col
     order = factor_inverse.shape[0]
     width = panel_right.shape[2]
-    whole = lax.all_to_all(panel_right, "col", split_axis=0, concat_axis=1, tiled=True)
+    whole = swap_blocks(panel_right, "col", 0, 1)
     solved = jnp.einsum("ij,bjk->bik", factor_inverse, whole, preferred_element_type=jnp.float32)
     column = lax.broadcasted_iota(jnp.int32, (1, 1, width), 2)
     keep = column < ranks.reshape(1, 1, 1)

time: 148 us -> 160 us (1.081)
  local copies, waits for them, and re-layouts: 6.37 us -> 17.7 us
    unnamed x3 -> x10, local copies, waits for them, and re-layouts: 1.94 us -> 11.9 us
where the time goes in v1:
time: 160 us; the launch traced here: 159 us
  waiting for transfers between devices  91.7 us (57%)
  local copies, waits for them, and re-layouts  17.7 us (11%)
  blocking collectives  15.8 us (10%)
  between operations  14.1 us (9%)
  starting transfers between devices  9.97 us (6%)
  matrix products  9.54 us (6%)
    all_gather x1, waiting for transfers between devices, body(): lax.all_gather(held, 'col', axis=0, tiled=True)  39.9 us
    all_gather x1, waiting for transfers between devices, body(): column_set = lax.all_gather(held, 'row', axis=0, tiled=True)  25.9 us
    all_to_all x1, blocking collectives, body(): lax.all_to_all(moved, ('row', 'col'), split_axis=0, concat_axis=0, tiled=...  15.8 us
    all_to_all x1, waiting for transfers between devices, body(): lax.all_to_all(pieces, ('row', 'col'), split_axis=0, concat_axis=0, tiled...  13.3 us
    unnamed x10, local copies, waits for them, and re-layouts  11.9 us
    all_to_all x1, waiting for transfers between devices, swap_blocks(): received = lax.all_to_all(jnp.stack(shards), axis, 0, 0)  11.9 us
    all_to_all x1, starting transfers between devices, swap_blocks(): received = lax.all_to_all(jnp.stack(shards), axis, 0, 0)  6.35 us
    dot_general x1, matrix products, body(): jnp.einsum('aik,bil->abkl', lax.all_gather(held, 'col', axis=0, tiled=Tru...  5.51 us
  transfers between devices with their start and end apart: 4, of which 4 were waited for; matrix products, arithmetic and copies ran while one was open for 1% of the time, Pallas kernels for 0%

profile of v1, /device:TPU:0, one launch (start us, length us, event | category | flops | bytes accessed | tf_op | source)
XLA Modules:
  0.0 159.0 jit_solution(2959239194299270479)
XLA Ops:
  6.5 1.4 bitcast_dynamic-update-slice_fusion.7
  8.0 1.4 bitcast_dynamic-update-slice_fusion.6
  9.4 1.4 bitcast_dynamic-update-slice_fusion.5
  10.8 1.4 bitcast_dynamic-update-slice_fusion.4
  12.2 1.4 bitcast_dynamic-update-slice_fusion.3
  13.6 1.4 bitcast_dynamic-update-slice_fusion.2
  15.1 1.4 bitcast_dynamic-update-slice_fusion.1
  16.5 1.4 bitcast_dynamic-update-slice_fusion
  17.9 6.4 %all-to-all-start = ((bf16[8,1,192,128]{3,2,1,0:T(8,128)(2,1)}), bf16[8,1,192,128]{3,2,1,0:T(8,128)(2,1)S(1)}, u32[]{:S(2)}, u32[]{:S(2)}) async-start(bf16[8,1,192,128]{3,2,1,0:T(8,128)(2,1)} %bitcast_dynamic-update-slice_fusion), calls=%async_computation | async-start | bytes 786432 | tf_op jit(solution)/shard_map/all_to_all | solution.py:9
  24.9 11.9 %all-to-all-done = bf16[8,1,192,128]{3,2,1,0:T(8,128)(2,1)S(1)} async-done(((bf16[8,1,192,128]{3,2,1,0:T(8,128)(2,1)}), bf16[8,1,192,128]{3,2,1,0:T(8,128)(2,1)S(1)}, u32[]{:S(2)}, u32[]{:S(2)}) %all-to-all-start) | async-done | bytes 393248 | tf_op jit(solution)/shard_map/all_to_all | solution.py:9
  36.8 0.0 copy-start
  36.8 4.0 %fusion.4 = bf16[1,1536,128]{1,2,0:T(8,128)(2,1)S(1)} fusion(bf16[1536,128]{1,0:T(8,128)(2,1)S(1)} %bitcast.49, bf16[1536,1536]{1,0:T(8,128)(2,1)} %param.6, pred[128]{0:T(512)(128)(4,1)S(1)} %iota_compare_fusion), kind=kOutput, calls=%fused_computation.6 | convolution fusion | flops 604372992 | bytes 5505152 | tf_op jit(solution)/shard_map/ij,bjk->bik/dot_general | solution.py:20
  40.8 0.9 copy.14
  41.7 3.5 %all-to-all-start.1 = ((bf16[32,48,128]{2,1,0:T(8,128)(2,1)}), bf16[32,48,128]{2,1,0:T(8,128)(2,1)S(1)}, u32[]{:S(2)}, u32[]{:S(2)}) async-start(bf16[32,48,128]{2,1,0:T(8,128)(2,1)} %bitcast.12), calls=%async_computation.1 | async-start | bytes 786432 | tf_op jit(solution)/shard_map/all_to_all | solution.py:25
  45.3 0.0 all-gather.3.cloned.1.call-start
  45.3 0.0 copy-done
  45.4 13.3 %all-to-all-done.1 = bf16[32,48,128]{2,1,0:T(8,128)(2,1)S(1)} async-done(((bf16[32,48,128]{2,1,0:T(8,128)(2,1)}), bf16[32,48,128]{2,1,0:T(8,128)(2,1)S(1)}, u32[]{:S(2)}, u32[]{:S(2)}) %all-to-all-start.1) | async-done | bytes 393248 | tf_op jit(solution)/shard_map/all_to_all | solution.py:25
  58.7 0.6 gather_fusion
  59.3 0.1 broadcast_select_fusion
  59.4 15.8 %all_to_all.15 = bf16[32,48,128]{2,1,0:T(8,128)(2,1)} all-to-all(bf16[32,48,128]{2,1,0:T(8,128)(2,1)S(1)} %broadcast_select_fusion), channel_id=1, replica_groups=mesh['row'=4,'col'=8] {'row','col'}, dimensions={0} | all-to-all | bytes 786432 | tf_op jit(solution)/shard_map/all_to_all | solution.py:27
  75.3 0.0 all-gather.3.cloned.1.call-update
  75.3 0.0 all-gather.5.cloned.1.call-start
  75.3 0.7 all-gather.5.cloned.1.call-update
  76.0 1.9 %copy.16 = f32[1,1,8,4,128,128]{4,5,2,3,1,0:T(8,128)S(1)} copy(f32[1,1,8,4,128,128]{5,4,3,2,1,0:T(8,128)} %param.9) | data formatting | bytes 4194304 | tf_op args[4]
  78.0 25.9 %all-gather.3.cloned.1.call-done = bf16[4,1536,128]{2,1,0:T(8,128)(2,1)} async-done(((bf16[1,1536,128]{2,1,0:T(8,128)(2,1)}), bf16[4,1536,128]{2,1,0:T(8,128)(2,1)}) %all-gather.3.cloned.1.call-update) | async-done | bytes 1572880 | tf_op jit(solution)/shard_map/all_gather | solution.py:29
  103.9 39.9 %all-gather.5.cloned.1.call-done = bf16[8,1536,128]{2,1,0:T(8,128)(2,1)} async-done(((bf16[1,1536,128]{2,1,0:T(8,128)(2,1)}), bf16[8,1536,128]{2,1,0:T(8,128)(2,1)}) %all-gather.5.cloned.1.call-update) | async-done | bytes 3145744 | tf_op jit(solution)/shard_map/all_gather | solution.py:32
  143.8 5.5 %bitcast_subtract_fusion = f32[1,1,8,4,128,128]{4,5,2,3,1,0:T(8,128)} fusion(f32[1,1,8,4,128,128]{4,5,2,3,1,0:T(8,128)S(1)} %copy.16, bf16[8,1536,128]{2,1,0:T(8,128)(2,1)} %all-gather.5.cloned.1.call-done, bf16[4,1536,128]{2,1,0:T(8,128)(2,1)} %all-gather.3.cloned.1.call-done), kind=kOutput, calls=%fused_computation.7 | convolution fusion | flops 1611137024 | bytes 8912896 | tf_op jit(solution)/shard_map/aik,bil->abkl/dot_general | solution.py:30
  149.3 2.9 %copy.17 = f32[1,1,8,4,128,128]{5,4,3,2,1,0:T(8,128)} copy(f32[1,1,8,4,128,128]{4,5,2,3,1,0:T(8,128)} %bitcast_subtract_fusion) | data formatting | bytes 4194304 | tf_op jit(solution)/shard_map/sub | solution.py:36
  (4 shorter events, 0.0 us)
Async XLA Ops:
  17.9 18.9 %all-to-all-start = ((bf16[8,1,192,128]{3,2,1,0:T(8,128)(2,1)}), bf16[8,1,192,128]{3,2,1,0:T(8,128)(2,1)S(1)}, u32[]{:S(2)}, u32[]{:S(2)}) async-start(bf16[8,1,192,128]{3,2,1,0:T(8,128)(2,1)} %bitcast_dynamic-update-slice_fusion), calls=%async_computation | async-start | bytes 786432 | tf_op jit(solution)/shard_map/all_to_all | solution.py:9
  36.8 8.6 %copy-start = (s32[32]{0:T(128)S(1)}, s32[32]{0:T(128)}, u32[]{:S(2)}) copy-start(s32[32]{0:T(128)} %param.8) | copy-start | bytes 388
  41.7 17.0 %all-to-all-start.1 = ((bf16[32,48,128]{2,1,0:T(8,128)(2,1)}), bf16[32,48,128]{2,1,0:T(8,128)(2,1)S(1)}, u32[]{:S(2)}, u32[]{:S(2)}) async-start(bf16[32,48,128]{2,1,0:T(8,128)(2,1)} %bitcast.12), calls=%async_computation.1 | async-start | bytes 786432 | tf_op jit(solution)/shard_map/all_to_all | solution.py:25
  45.3 58.6 %all-gather.3.cloned.1.call-start = ((), (), s32[]{:S(2)}) async-start(), calls=%async_computation.3 | async-start | bytes 1966080 | tf_op jit(solution)/shard_map/all_gather | solution.py:29
  75.3 68.5 %all-gather.5.cloned.1.call-start = ((), (), s32[]{:S(2)}) async-start(), calls=%async_computation.4 | async-start | bytes 3538944 | tf_op jit(solution)/shard_map/all_gather | solution.py:32
Sparse Core Ops, SparseCore 0:
  75.4 28.4 all-gather.2
  105.5 38.2 all-gather.4
